TPU v7x, 256 devices: a whole 4x4x8 slice. The times are simulated.
256 devices in a mesh: rows: 128 (over z, y, x), cols: 2 (over core).
Axes of the slice: x: 4, y: 4, z: 8, core: 2. Of those that a mesh axis runs over, the one named last changes fastest.
Arguments:
- design: float32 [131072, 512], P('rows', 'cols'), may hold values from -24 to 24
- signs: int32 [131072], P('rows'), may hold values from -1 to 1, as said below
- kept: int32 [8192], replicated, may hold values from 0 to 131071, as said below
Outputs:
- sketch: float32 [8192, 512], P('rows', 'cols')
- factor: float32 [512, 512], P(None, 'cols')
Inputs may be any that keep to these rules, and one draw needn't show every extreme that they name: `signs`: each entry is +1 or -1. `kept`: distinct and increasing.
All inputs are finite; a program needn't handle non-finite values.
Results may differ from a plain program's by a relative error of at most 0.0003.
Values sent between devices are 32-bit elements; how exact they have to be, the bound alone decides.
No kernel may reach another device: no remote copies, remote signals or barrier semaphores. Data moves between devices by JAX's collectives and lax.ppermute only.
A program may use at most 64 MiB of HBM per device.

v0:
```python
import math
import jax
import jax.numpy as jnp
from jax import lax
from jax.sharding import Mesh
from jax.sharding import PartitionSpec as P

ROWS = ("rows_0", "rows_1", "rows_2")


def sum_by_axis(so_far, axes):
    for axis in axes:
        so_far = lax.psum_scatter(so_far, axis, scatter_dimension=0, tiled=True)
    return so_far


def laid_out(parts, dim):
    dims = list(parts.shape[1:])
    dims[dim] *= parts.shape[0]
    return jnp.moveaxis(parts, 0, dim).reshape(dims)


def copy_for_each(shard, axis):
    length = lax.axis_size(axis)
    return lax.all_to_all(
        jnp.broadcast_to(shard[None], (length, *shard.shape)), axis, 0, 0, tiled=True
    )


def gathered_copies(shard, axis, dim):
    return laid_out(copy_for_each(shard, axis), dim)


def hadamard(order):
    matrix = jnp.ones((1, 1), jnp.float32)
    base = jnp.array([[1.0, 1.0], [1.0, -1.0]], jnp.float32)
    while matrix.shape[0] < order:
        matrix = jnp.kron(matrix, base)
    return matrix


def bit_parity(value):
    folded = value
    for amount in (16, 8, 4, 2, 1):
        folded = jnp.bitwise_xor(folded, jnp.right_shift(folded, amount))
    return jnp.bitwise_and(folded, 1)


def local_transform(flipped):
    length, width = flipped.shape
    outer = length // 128
    inner_table = hadamard(128)
    outer_table = hadamard(outer)
    blocks = flipped.reshape(outer, 128, width)
    mixed = jnp.einsum("pb,abc->apc", inner_table, blocks, precision=lax.Precision.HIGHEST)
    mixed = jnp.einsum("qa,apc->qpc", outer_table, mixed, precision=lax.Precision.HIGHEST)
    return mixed.reshape(length, width)


def signed_rows(transformed, kept_part, device_row, total_rows):
    length = transformed.shape[0]
    kept_blocks = kept_part // length
    offsets = kept_part - kept_blocks * length
    parity = bit_parity(jnp.bitwise_and(kept_blocks, device_row))
    factor = (1.0 - 2.0 * parity.astype(jnp.float32)) / math.sqrt(total_rows)
    return jnp.take(transformed, offsets, axis=0) * factor[:, None]


def body(design, signs, kept):
    flipped = design * signs.astype(jnp.float32)[:, None]
    transformed = local_transform(flipped)
    device_row = lax.axis_index(ROWS)
    groups = lax.axis_size(ROWS)
    length = transformed.shape[0]
    widths = transformed.shape[1]
    total_rows = length * groups
    sketch = sum_by_axis(signed_rows(transformed, kept, device_row, total_rows), ROWS)
    column = lax.axis_index("cols")
    whole = gathered_copies(sketch, "cols", 1)
    kept_total = kept.shape[0]
    partial_gram = jnp.dot(
        whole.T, whole, precision=lax.Precision.HIGHEST, preferred_element_type=jnp.float32
    )
    gram = lax.psum(partial_gram, ROWS) / kept_total
    factor = jnp.linalg.cholesky(gram).T
    return (sketch, lax.dynamic_slice_in_dim(factor, column * widths, widths, 1))


def solution(mesh):
    torus = Mesh(
        mesh.devices.reshape(8, 4, 4, mesh.shape["cols"]), ("rows_0", "rows_1", "rows_2", "cols")
    )
    return jax.shard_map(
        body,
        mesh=torus,
        in_specs=(P(ROWS, "cols"), P(ROWS), P()),
        out_specs=(P(ROWS, "cols"), P(None, "cols")),
        check_vma=False,
    )
```

profile of v0, /device:TPU:2, one launch (start us, length us, event | category | flops | bytes accessed | tf_op | source)
XLA Modules:
  0.0 540.0 jit_solution(2784497924892284188)
XLA Ops:
  7.2 0.8 broadcast_multiply_fusion.7
  13.1 0.9 broadcast_multiply_fusion.2
  14.7 3.0 broadcast_multiply_fusion
  17.7 4.0 reshape.195
  21.9 1.8 convolution_bitcast_fusion
  24.2 1.0 fusion.21
  25.6 31.4 %gather_fusion = f32[8192,256]{1,0:T(8,128)} fusion(f32[1024,256]{1,0:T(8,128)S(1)} %bitcast.45, s32[8192]{0:T(1024)S(1)} %broadcast_clamp_fusion), kind=kCustom, calls=%fused_computation | custom fusion | bytes 16809984 | tf_op jit(solution)/shard_map/jit(_take)/gather | solution.py:66
  57.0 9.9 %select_multiply_fusion = f32[8192,256]{1,0:T(8,128)} fusion(f32[8192,256]{1,0:T(8,128)} %gather_fusion, f32[8192]{0:T(1024)S(1)} %fusion.19, pred[8192]{0:T(1024)(128)(4,1)S(1)} %compare_and_fusion), kind=kLoop, calls=%fused_computation.1 | loop fusion | flops 4194304 | bytes 16818176 | tf_op jit(solution)/shard_map/mul | solution.py:66
  66.9 97.9 %reduce-scatter.4.cloned.1.call-done = f32[1024,256]{1,0:T(8,128)} async-done(((f32[8192,256]{1,0:T(8,128)}), f32[1024,256]{1,0:T(8,128)}) %reduce-scatter.4.cloned.1.call-update) | async-done | bytes 1048592 | tf_op jit(solution)/shard_map/reduce_scatter | solution.py:13
  165.0 27.3 %reduce-scatter.6.cloned.1.call-done = f32[256,256]{1,0:T(8,128)} async-done(((f32[1024,256]{1,0:T(8,128)}), f32[256,256]{1,0:T(8,128)}) %reduce-scatter.6.cloned.1.call-update) | async-done | bytes 262160 | tf_op jit(solution)/shard_map/reduce_scatter | solution.py:13
  192.3 24.3 %reduce-scatter.8.cloned.1.call-done = f32[64,256]{1,0:T(8,128)} async-done(((f32[256,256]{1,0:T(8,128)}), f32[64,256]{1,0:T(8,128)}) %reduce-scatter.8.cloned.1.call-update) | async-done | bytes 65552 | tf_op jit(solution)/shard_map/reduce_scatter | solution.py:13
  217.4 3.8 all_to_all.5
  221.3 2.1 fusion.22
  223.4 222.7 %all-reduce.3.cloned.1.call-done = f32[512,512]{0,1:T(8,128)} async-done(((f32[512,512]{0,1:T(8,128)}), f32[512,512]{0,1:T(8,128)}) %all-reduce.3.cloned.1.call-update) | async-done | bytes 1048592 | tf_op jit(solution)/shard_map/psum | solution.py:84
  446.1 1.3 broadcast_multiply_fusion.1
  447.7 1.5 fusion
  449.2 11.7 %cholesky.104 = f32[128,128]{1,0:T(8,128)S(1)} custom-call(f32[128,128]{1,0:T(8,128)S(1)} %cholesky.266), custom_call_target="Cholesky" | custom-call | tf_op jit(solution)/shard_map/jit(cholesky)/cholesky | solution.py:85
  461.1 9.8 %custom-call.27 = f32[1,128,128]{1,2,0:T(8,128)S(1)} custom-call(f32[1,128,128]{2,1,0:T(8,128)S(1)} %get-tuple-element.17), custom_call_target="InvertDiagBlocksLowerTriangular" | custom-call | tf_op jit(solution)/shard_map/jit(cholesky)/cholesky | solution.py:85
  471.6 11.7 %cholesky.217 = f32[128,128]{1,0:T(8,128)S(1)} custom-call(f32[128,128]{1,0:T(8,128)S(1)} %cholesky.270), custom_call_target="Cholesky" | custom-call | tf_op jit(solution)/shard_map/jit(cholesky)/cholesky | solution.py:85
  483.3 9.9 %custom-call.28 = f32[1,128,128]{1,2,0:T(8,128)S(1)} custom-call(f32[1,128,128]{2,1,0:T(8,128)S(1)} %get-tuple-element.14), custom_call_target="InvertDiagBlocksLowerTriangular" | custom-call | tf_op jit(solution)/shard_map/jit(cholesky)/cholesky | solution.py:85
  494.0 11.7 %cholesky.238 = f32[128,128]{1,0:T(8,128)S(1)} custom-call(f32[128,128]{1,0:T(8,128)S(1)} %cholesky.275), custom_call_target="Cholesky" | custom-call | tf_op jit(solution)/shard_map/jit(cholesky)/cholesky | solution.py:85
  505.7 9.8 %custom-call.29 = f32[1,128,128]{1,2,0:T(8,128)S(1)} custom-call(f32[1,128,128]{2,1,0:T(8,128)S(1)} %get-tuple-element.11), custom_call_target="InvertDiagBlocksLowerTriangular" | custom-call | tf_op jit(solution)/shard_map/jit(cholesky)/cholesky | solution.py:85
  516.1 11.7 %cholesky.255 = f32[128,128]{1,0:T(8,128)S(1)} custom-call(f32[128,128]{1,0:T(8,128)S(1)} %convolution_subtract_fusion.2), custom_call_target="Cholesky" | custom-call | tf_op jit(solution)/shard_map/jit(cholesky)/cholesky | solution.py:85
  532.5 1.0 copy.20
  (49 shorter events, 12.4 us)
Async XLA Ops:
  7.2 14.5 %copy-start = (f32[1024,256]{1,0:T(8,128)S(1)}, f32[1024,256]{1,0:T(8,128)}, u32[]{:S(2)}) copy-start(f32[1024,256]{1,0:T(8,128)} %param.5) | copy-start | bytes 3145732
  7.2 157.7 %reduce-scatter.4.cloned.1.call-start = ((), (), s32[]{:S(2)}) async-start(), calls=%async_computation.4 | async-start | bytes 9437184 | tf_op jit(solution)/shard_map/reduce_scatter | solution.py:13
  17.7 7.9 %copy-start.1 = (s32[8192]{0:T(1024)S(1)}, s32[8192]{0:T(1024)}, u32[]{:S(2)}) copy-start(s32[8192]{0:T(1024)} %param.7) | copy-start | bytes 98308
  66.9 125.3 %reduce-scatter.6.cloned.1.call-start = ((), (), s32[]{:S(2)}) async-start(), calls=%async_computation.5 | async-start | bytes 1310720 | tf_op jit(solution)/shard_map/reduce_scatter | solution.py:13
  164.9 51.7 %reduce-scatter.8.cloned.1.call-start = ((), (), s32[]{:S(2)}) async-start(), calls=%async_computation.6 | async-start | bytes 327680 | tf_op jit(solution)/shard_map/reduce_scatter | solution.py:13
  192.3 253.8 %all-reduce.3.cloned.1.call-start = ((), (), s32[]{:S(2)}) async-start(), calls=%async_computation.7 | async-start | bytes 2097152 | tf_op jit(solution)/shard_map/psum | solution.py:84
Sparse Core Ops, SparseCore 0:
  67.0 97.8 reduce-scatter.3
  167.4 24.7 reduce-scatter.5
  195.5 21.0 reduce-scatter.7
  223.5 222.5 all-reduce.2
where the time goes:
time: 541 us; the launch traced here: 540 us
  waiting for transfers between devices  372 us (69%)
  other arithmetic  101 us (19%)
  local copies, waits for them, and re-layouts  39.6 us (7%)
  between operations  16.6 us (3%)
  matrix products  6.71 us (1%)
    psum x1, waiting for transfers between devices, body(): gram = lax.psum(partial_gram, ROWS) / kept_total  223 us
    reduce_scatter x3, waiting for transfers between devices, sum_by_axis(): so_far = lax.psum_scatter(so_far, axis, scatter_dimension=0, tiled=True)  149 us
    another operation x14, other arithmetic, body(): factor = jnp.linalg.cholesky(gram).T  78.6 us
    gather x1, local copies, waits for them, and re-layouts, signed_rows(): return jnp.take(transformed, offsets, axis=0) * factor[:, None]  31.4 us
  transfers between devices with their start and end apart: 4, of which 4 were waited for; matrix products, arithmetic and copies ran while one was open for 0% of the time, Pallas kernels for 0%

commit v1 on v0

--- a/solution.py
+++ b/solution.py
@@ -6,6 +6,12 @@
 from jax.sharding import PartitionSpec as P
 
 ROWS = ("rows_0", "rows_1", "rows_2")
+
+
+def _place_meshes(v0, axis_key, peer_axis):
+    for dd in (axis_key, peer_axis):
+        v0 = lax.psum(v0, axis_name=dd)
+    return v0
 
 
 def sum_by_axis(so_far, axes):
@@ -81,7 +87,9 @@
     partial_gram = jnp.dot(
         whole.T, whole, precision=lax.Precision.HIGHEST, preferred_element_type=jnp.float32
     )
-    gram = lax.psum(partial_gram, ROWS) / kept_total
+    gram = (
+        _place_meshes(partial_gram, axis_key=("rows_1", "rows_2"), peer_axis="rows_0") / kept_total
+    )
     factor = jnp.linalg.cholesky(gram).T
     return (sketch, lax.dynamic_slice_in_dim(factor, column * widths, widths, 1))
 

time: 541 us -> 494 us (0.913)
  waiting for transfers between devices: 372 us -> 326 us
    psum x1 -> x2, waiting for transfers between devices: 223 us -> 176 us  [_place_meshes(): v0 = lax.psum(v0, axis_name=dd)]
  transfers between devices with their start and end apart: 4 -> 5, of which waited for: 4 -> 5; matrix products, arithmetic and copies ran while one was open for 0% -> 0% of each run, Pallas kernels for 0% -> 0%
where the time goes in v1:
time: 494 us
  waiting for transfers between devices  326 us (66%)
  other arithmetic  101 us (20%)
  local copies, waits for them, and re-layouts  39.6 us (8%)
  between operations  16.6 us (3%)
  matrix products  6.71 us (1%)
    psum x2, waiting for transfers between devices, _place_meshes(): v0 = lax.psum(v0, axis_name=dd)  176 us
    reduce_scatter x3, waiting for transfers between devices, sum_by_axis(): so_far = lax.psum_scatter(so_far, axis, scatter_dimension=0, tiled=True)  149 us
    another operation x14, other arithmetic, body(): factor = jnp.linalg.cholesky(gram).T  78.6 us
    gather x1, local copies, waits for them, and re-layouts, signed_rows(): return jnp.take(transformed, offsets, axis=0) * factor[:, None]  31.4 us
    mul x1, other arithmetic, signed_rows(): return jnp.take(transformed, offsets, axis=0) * factor[:, None]  9.89 us
  transfers between devices with their start and end apart: 5, of which 5 were waited for; matrix products, arithmetic and copies ran while one was open for 0% of the time, Pallas kernels for 0%

profile of v1, /device:TPU:2, one launch (start us, length us, event | category | flops | bytes accessed | tf_op | source)
XLA Modules:
  0.0 493.6 jit_solution(15989390673865188756)
XLA Ops:
  13.1 0.9 broadcast_multiply_fusion.2
  14.7 3.0 broadcast_multiply_fusion
  17.7 4.0 reshape.195
  21.9 1.8 convolution_bitcast_fusion
  24.2 1.0 fusion.21
  25.6 31.4 %gather_fusion = f32[8192,256]{1,0:T(8,128)} fusion(f32[1024,256]{1,0:T(8,128)S(1)} %bitcast.45, s32[8192]{0:T(1024)S(1)} %broadcast_clamp_fusion), kind=kCustom, calls=%fused_computation | custom fusion | bytes 16809984 | tf_op jit(solution)/shard_map/jit(_take)/gather | solution.py:72
  57.0 9.9 %select_multiply_fusion = f32[8192,256]{1,0:T(8,128)} fusion(f32[8192,256]{1,0:T(8,128)} %gather_fusion, f32[8192]{0:T(1024)S(1)} %fusion.19, pred[8192]{0:T(1024)(128)(4,1)S(1)} %compare_and_fusion), kind=kLoop, calls=%fused_computation.1 | loop fusion | flops 4194304 | bytes 16818176 | tf_op jit(solution)/shard_map/mul | solution.py:72
  66.9 97.9 %reduce-scatter.4.cloned.1.call-done = f32[1024,256]{1,0:T(8,128)} async-done(((f32[8192,256]{1,0:T(8,128)}), f32[1024,256]{1,0:T(8,128)}) %reduce-scatter.4.cloned.1.call-update) | async-done | bytes 1048592 | tf_op jit(solution)/shard_map/reduce_scatter | solution.py:19
  165.0 27.3 %reduce-scatter.6.cloned.1.call-done = f32[256,256]{1,0:T(8,128)} async-done(((f32[1024,256]{1,0:T(8,128)}), f32[256,256]{1,0:T(8,128)}) %reduce-scatter.6.cloned.1.call-update) | async-done | bytes 262160 | tf_op jit(solution)/shard_map/reduce_scatter | solution.py:19
  192.3 24.3 %reduce-scatter.8.cloned.1.call-done = f32[64,256]{1,0:T(8,128)} async-done(((f32[256,256]{1,0:T(8,128)}), f32[64,256]{1,0:T(8,128)}) %reduce-scatter.8.cloned.1.call-update) | async-done | bytes 65552 | tf_op jit(solution)/shard_map/reduce_scatter | solution.py:19
  217.4 3.8 all_to_all.5
  221.3 2.1 fusion.22
  223.6 98.2 %all-reduce.4.cloned.1.call-done = f32[512,512]{0,1:T(8,128)} async-done(((f32[512,512]{0,1:T(8,128)}), f32[512,512]{0,1:T(8,128)}) %all-reduce.4.cloned.1.call-update) | async-done | bytes 1048592 | tf_op jit(solution)/shard_map/psum | solution.py:13
  321.8 77.8 %all-reduce.6.cloned.1.call-done = f32[512,512]{0,1:T(8,128)} async-done(((f32[512,512]{0,1:T(8,128)}), f32[512,512]{0,1:T(8,128)}) %all-reduce.6.cloned.1.call-update) | async-done | bytes 1048592 | tf_op jit(solution)/shard_map/psum | solution.py:13
  399.6 1.3 broadcast_multiply_fusion.1
  401.3 1.5 fusion
  402.8 11.7 %cholesky.104 = f32[128,128]{1,0:T(8,128)S(1)} custom-call(f32[128,128]{1,0:T(8,128)S(1)} %cholesky.266), custom_call_target="Cholesky" | custom-call | tf_op jit(solution)/shard_map/jit(cholesky)/cholesky | solution.py:93
  414.7 9.8 %custom-call.27 = f32[1,128,128]{1,2,0:T(8,128)S(1)} custom-call(f32[1,128,128]{2,1,0:T(8,128)S(1)} %get-tuple-element.17), custom_call_target="InvertDiagBlocksLowerTriangular" | custom-call | tf_op jit(solution)/shard_map/jit(cholesky)/cholesky | solution.py:93
  425.1 11.7 %cholesky.217 = f32[128,128]{1,0:T(8,128)S(1)} custom-call(f32[128,128]{1,0:T(8,128)S(1)} %cholesky.270), custom_call_target="Cholesky" | custom-call | tf_op jit(solution)/shard_map/jit(cholesky)/cholesky | solution.py:93
  436.9 10.0 %custom-call.28 = f32[1,128,128]{1,2,0:T(8,128)S(1)} custom-call(f32[1,128,128]{2,1,0:T(8,128)S(1)} %get-tuple-element.14), custom_call_target="InvertDiagBlocksLowerTriangular" | custom-call | tf_op jit(solution)/shard_map/jit(cholesky)/cholesky | solution.py:93
  447.6 11.7 %cholesky.238 = f32[128,128]{1,0:T(8,128)S(1)} custom-call(f32[128,128]{1,0:T(8,128)S(1)} %cholesky.275), custom_call_target="Cholesky" | custom-call | tf_op jit(solution)/shard_map/jit(cholesky)/cholesky | solution.py:93
  459.3 9.8 %custom-call.29 = f32[1,128,128]{1,2,0:T(8,128)S(1)} custom-call(f32[1,128,128]{2,1,0:T(8,128)S(1)} %get-tuple-element.11), custom_call_target="InvertDiagBlocksLowerTriangular" | custom-call | tf_op jit(solution)/shard_map/jit(cholesky)/cholesky | solution.py:93
  469.7 11.7 %cholesky.255 = f32[128,128]{1,0:T(8,128)S(1)} custom-call(f32[128,128]{1,0:T(8,128)S(1)} %convolution_subtract_fusion.2), custom_call_target="Cholesky" | custom-call | tf_op jit(solution)/shard_map/jit(cholesky)/cholesky | solution.py:93
  486.1 1.0 copy.20
  (52 shorter events, 13.5 us)
Async XLA Ops:
  7.2 14.5 %copy-start = (f32[1024,256]{1,0:T(8,128)S(1)}, f32[1024,256]{1,0:T(8,128)}, u32[]{:S(2)}) copy-start(f32[1024,256]{1,0:T(8,128)} %param.5) | copy-start | bytes 3145732
  7.2 157.7 %reduce-scatter.4.cloned.1.call-start = ((), (), s32[]{:S(2)}) async-start(), calls=%async_computation.4 | async-start | bytes 9437184 | tf_op jit(solution)/shard_map/reduce_scatter | solution.py:19
  17.7 7.9 %copy-start.1 = (s32[8192]{0:T(1024)S(1)}, s32[8192]{0:T(1024)}, u32[]{:S(2)}) copy-start(s32[8192]{0:T(1024)} %param.7) | copy-start | bytes 98308
  66.9 125.3 %reduce-scatter.6.cloned.1.call-start = ((), (), s32[]{:S(2)}) async-start(), calls=%async_computation.5 | async-start | bytes 1310720 | tf_op jit(solution)/shard_map/reduce_scatter | solution.py:19
  164.9 51.7 %reduce-scatter.8.cloned.1.call-start = ((), (), s32[]{:S(2)}) async-start(), calls=%async_computation.6 | async-start | bytes 327680 | tf_op jit(solution)/shard_map/reduce_scatter | solution.py:19
  192.3 129.5 %all-reduce.4.cloned.1.call-start = ((), (), s32[]{:S(2)}) async-start(), calls=%async_computation.7 | async-start | bytes 2097152 | tf_op jit(solution)/shard_map/psum | solution.py:13
  223.4 176.3 %all-reduce.6.cloned.1.call-start = ((), (), s32[]{:S(2)}) async-start(), calls=%async_computation.8 | async-start | bytes 2097152 | tf_op jit(solution)/shard_map/psum | solution.py:13
Sparse Core Ops, SparseCore 0:
  67.0 97.8 reduce-scatter.3
  167.4 24.7 reduce-scatter.5
  195.5 21.0 reduce-scatter.7
  223.5 98.2 all-reduce.3
  324.0 75.6 all-reduce.5
